TPU v7x, 32 devices: a whole 2x2x4 slice. The times are simulated.
32 devices in a mesh: wide: 8 (over z, core), narrow: 4 (over y, x).
Axes of the slice: x: 2, y: 2, z: 4, core: 2. Of those that a mesh axis runs over, the one named last changes fastest.
Arguments:
- amplitudes: float32 [4, 64, 640, 640], P(None, 'wide', None, 'narrow'), may hold values from -6 to 6
- cycle_block: float32 [64, 640, 4, 640], P('wide', 'narrow'), may hold values from -0.078125 to 0.078125
- occupied_irreps: int32 [64], replicated, may hold values from 0 to 7, as said below
- virtual_irreps: int32 [640], replicated, may hold values from 0 to 7, as said below
- slab_orbitals: int32 [4], replicated, may hold values from 0 to 63, as said below
Outputs:
- cycle_residual: float32 [4, 4, 640, 640], P(None, None, 'narrow', 'wide')
Inputs may be any that keep to these rules, and one draw needn't show every extreme that they name: `occupied_irreps`: nondecreasing; every irrep 0 to 7 labels at least 4 orbitals. `virtual_irreps`: nondecreasing; every irrep 0 to 7 labels at least 64 orbitals. `slab_orbitals`: distinct occupied orbital indices in increasing order; the last is 63.
All inputs are finite; a program needn't handle non-finite values.
Results may differ from a plain program's by a relative error of at most 0.0003.
Values sent between devices are 32-bit elements; how exact they have to be, the bound alone decides.
A program may use at most 192 MiB of HBM per device.

v0:
```python
import functools

import jax
import jax.numpy as jnp
from jax import lax
from jax.experimental import pallas as pl
from jax.experimental.pallas import tpu as pltpu
from jax.sharding import PartitionSpec as P

IRREPS = 8
ROWS = 8
FEWEST = 64


def split(x):
    high = x.astype(jnp.bfloat16)
    low = (x - high.astype(jnp.float32)).astype(jnp.bfloat16)
    return high, low


def mm(x, y):
    return jnp.dot(x, y, preferred_element_type=jnp.float32)


def contract(cap, wide, tab, a_ref, w_ref, hc_row, hc_col, hb_row, out_ref, acc, rows):
    k = pl.program_id(0)
    n_k = pl.num_programs(0)
    ni = a_ref.shape[0]
    nb = w_ref.shape[3]
    bw = nb // wide
    hk = tab[ni + k]
    base = ni + n_k
    first, last = tab[base + IRREPS], tab[base + IRREPS + 1]
    c_labels = hc_row[...]
    for i in range(ni):
        g = tab[i] ^ hk

        def pick(h, kept):
            block = a_ref[i, 0, pl.ds(pl.multiple_of(tab[base + (h ^ g)], ROWS), cap), :]
            return jnp.where(c_labels == h, block, kept)

        rows[i * cap : (i + 1) * cap, :] = lax.fori_loop(
            first, last + 1, pick, jnp.zeros((cap, a_ref.shape[3]), jnp.float32)
        )
    l_hi, l_lo = split(rows[...])
    labels = hc_col[...] ^ hb_row[...]
    w_all = jnp.swapaxes(w_ref[0], 0, 1)
    for j in range(ni):
        w = jnp.where(labels == (tab[j] ^ hk), w_all[j], 0.0)
        w_hi, w_lo = split(w)
        term = mm(l_hi, w_hi) + mm(l_hi, w_lo) + mm(l_lo, w_hi)

        @pl.when(k == 0)
        def _():
            acc[j] = term

        @pl.when(k > 0)
        def _():
            acc[j] += term

    @pl.when(k == n_k - 1)
    def _():
        for j in range(ni):
            turned = acc[j].T
            for w in range(wide):
                out_ref[(w * ni + j) * bw : (w * ni + j + 1) * bw, :] = turned[w * bw : (w + 1) * bw]


def unpack(cap, tab, g_ref, hb_row, out_ref, buf):
    ni, _, na, bw = out_ref.shape
    buf[...] = jnp.zeros_like(buf)
    first, last, a0 = (tab[ni + 3 * IRREPS + n] for n in range(3))
    labels = hb_row[...]
    at = a0 + lax.broadcasted_iota(jnp.int32, (na, bw), 0)
    for j in range(ni):
        turned = g_ref[j * bw : (j + 1) * bw, :].T
        for i in range(ni):
            buf[na : na + cap, :] = turned[i * cap : (i + 1) * cap]
            g = tab[i] ^ tab[j]

            def place(h, kept):
                block = h ^ g
                start = jnp.clip(na + a0 - tab[ni + block], 0, na + cap)
                low, high = tab[ni + IRREPS + block], tab[ni + 2 * IRREPS + block]
                use = (labels == h) & (at >= low) & (at < high)
                return jnp.where(use, buf[pl.ds(pl.multiple_of(start, ROWS), na), :], kept)

            out_ref[i, j] = lax.fori_loop(first, last + 1, place, jnp.zeros((na, bw), jnp.float32))


def local(amplitudes, cycle_block, occupied_irreps, virtual_irreps, slab_orbitals):
    ni, n_k, va, nc = amplitudes.shape
    vb = cycle_block.shape[3]
    wide, narrow = lax.axis_size("wide"), lax.axis_size("narrow")
    wide_pos, narrow_pos = lax.axis_index("wide"), lax.axis_index("narrow")
    bw, na = vb // wide, va // narrow
    most = va - (IRREPS - 1) * FEWEST
    cap = most // 2

    slab = jnp.sum(
        jnp.where(
            jnp.arange(occupied_irreps.shape[0], dtype=jnp.int32)[None, :] == slab_orbitals[:, None],
            occupied_irreps[None, :],
            0,
        ),
        axis=1,
    )
    occ_part = lax.dynamic_slice_in_dim(occupied_irreps, wide_pos * n_k, n_k)
    c_part = lax.dynamic_slice_in_dim(virtual_irreps, narrow_pos * nc, nc)
    b_part = lax.dynamic_slice_in_dim(virtual_irreps, wide_pos * bw, bw)
    names = jnp.arange(IRREPS, dtype=jnp.int32)
    starts = jnp.sum((virtual_irreps[None, :] < names[:, None]).astype(jnp.int32), axis=1)
    aligned = starts // ROWS * ROWS
    ends = jnp.concatenate([starts[1:], jnp.full((1,), va, jnp.int32)])

    def part(offset):
        packed = jnp.minimum(aligned + offset, va - cap)
        tab = jnp.concatenate([slab, occ_part, packed, c_part[:1], c_part[-1:]])
        partial_sums = pl.pallas_call(
            functools.partial(contract, cap, wide),
            out_shape=jax.ShapeDtypeStruct((ni * vb, ni * cap), jnp.float32),
            grid_spec=pltpu.PrefetchScalarGridSpec(
                num_scalar_prefetch=1,
                grid=(n_k,),
                in_specs=[
                    pl.BlockSpec((ni, 1, va, nc), lambda k, t: (0, k, 0, 0)),
                    pl.BlockSpec((1, nc, ni, vb), lambda k, t: (k, 0, 0, 0)),
                    pl.BlockSpec((1, nc), lambda k, t: (0, 0)),
                    pl.BlockSpec((nc, 1), lambda k, t: (0, 0)),
                    pl.BlockSpec((1, vb), lambda k, t: (0, 0)),
                ],
                out_specs=pl.BlockSpec((ni * vb, ni * cap), lambda k, t: (0, 0)),
                scratch_shapes=[
                    pltpu.VMEM((ni, ni * cap, vb), jnp.float32),
                    pltpu.VMEM((ni * cap, nc), jnp.float32),
                ],
            ),
            compiler_params=pltpu.CompilerParams(vmem_limit_bytes=60 * 2**20),
        )(tab, amplitudes, cycle_block, c_part[None, :], c_part[:, None], virtual_irreps[None, :])
        mine = lax.psum_scatter(partial_sums, ("wide", "narrow"), scatter_dimension=0, tiled=True)
        summed = lax.all_gather(mine, "narrow", axis=0, tiled=True)
        low = jnp.maximum(aligned + offset, starts)
        high = jnp.minimum(aligned + offset + cap, ends)
        tab = jnp.concatenate([slab, packed, low, high, b_part[:1], b_part[-1:], (narrow_pos * na)[None]])
        return pl.pallas_call(
            functools.partial(unpack, cap),
            out_shape=jax.ShapeDtypeStruct((ni, ni, na, bw), jnp.float32),
            grid_spec=pltpu.PrefetchScalarGridSpec(
                num_scalar_prefetch=1,
                grid=(1,),
                in_specs=[
                    pl.BlockSpec((ni * bw, ni * cap), lambda k, t: (0, 0)),
                    pl.BlockSpec((1, bw), lambda k, t: (0, 0)),
                ],
                out_specs=pl.BlockSpec((ni, ni, na, bw), lambda k, t: (0, 0, 0, 0)),
                scratch_shapes=[pltpu.VMEM((2 * na + cap, bw), jnp.float32)],
            ),
        )(tab, summed, b_part[None, :])

    first = part(0)
    return lax.cond(jnp.max(ends - aligned) > cap, lambda x: x + part(cap), lambda x: x, first)


def solution(mesh):
    placed = (P(None, "wide", None, "narrow"), P("wide", "narrow", None, None), P(), P(), P())
    return jax.shard_map(
        local,
        mesh=mesh,
        in_specs=placed,
        out_specs=P(None, None, "narrow", "wide"),
        check_vma=False,
    )
```

profile of v0, /device:TPU:0, one launch (start us, length us, event | category | flops | bytes accessed | tf_op | source)
XLA Modules:
  0.0 210.6 jit_solution(9640255009092216787)
XLA Ops:
  6.5 0.0 reduce-scatter.5.cloned.1.call-start
  6.5 0.8 convert_reduce_fusion
  7.3 1.3 broadcast_in_dim.52.hb_row
  8.6 0.8 dynamic_slice.11
  9.4 0.7 dynamic_slice.10
  10.1 0.9 select_reduce_fusion
  11.0 0.1 slice.27
  11.0 0.7 fusion.4
  11.7 0.1 add_minimum_fusion.2
  11.8 0.7 pad_add_fusion
  12.5 0.8 copy.16.hc_col
  13.2 19.1 %copy.15.a_ref = f32[4,8,640,160]{3,2,1,0:T(8,128)} copy(f32[4,8,640,160]{2,3,1,0:T(8,128)} %param.7) | data formatting | bytes 26214400 | tf_op args[0]
  32.3 2.0 concatenate.17.tab
  34.3 45.8 %shard_map.57 = f32[2560,384]{1,0:T(8,128)} custom-call(s32[22]{0:T(128)} %concatenate.17.tab, f32[4,8,640,160]{3,2,1,0:T(8,128)} %copy.15.a_ref, f32[8,160,4,640]{3,2,1,0:T(4,128)} %w_ref.1, s32[1,160]{1,0:T(1,128)S(1)} %bitcast.10, s32[160,1]{1,0:T(8,128)} %copy.16.hc_col, s32[1,640]{1,0:T(1,128)} %broadcast_in_dim.52.hb_row), custom_call_target="tpu_custom_call" | custom-call | tf_op jit(solution)/shard_map/pallas_call | solution.py:119
  80.1 0.0 copy-start.1
  80.1 0.0 reduce-scatter.5.cloned.1.call-update
  80.1 0.7 copy-done.1
  80.8 0.1 dynamic_slice.9
  81.5 0.6 fusion.5
  82.1 2.0 concatenate.16.tab
  84.0 0.6 dynamic-slice_bitcast_fusion.hb_row
  84.6 103.5 %reduce-scatter.5.cloned.1.call-done = f32[80,384]{1,0:T(8,128)} async-done(((f32[2560,384]{1,0:T(8,128)}), f32[80,384]{1,0:T(8,128)}) %reduce-scatter.5.cloned.1.call-update) | async-done | bytes 122896 | tf_op jit(solution)/shard_map/reduce_scatter | solution.py:140
  188.1 11.7 %all_gather.6.g_ref = f32[320,384]{1,0:T(8,128)} all-gather(f32[80,384]{1,0:T(8,128)} %reduce-scatter.5.cloned.1.call-done), channel_id=1, replica_groups=mesh['wide'=8,'narrow'=4] {'narrow'}, dimensions={0}, use_global_device_ids=true | all-gather | bytes 614400 | tf_op jit(solution)/shard_map/all_gather | solution.py:141
  199.8 2.8 %shard_map.58 = f32[4,4,160,80]{3,2,1,0:T(8,128)S(1)} custom-call(s32[31]{0:T(128)} %concatenate.16.tab, f32[320,384]{1,0:T(8,128)} %all_gather.6.g_ref, s32[1,80]{1,0:T(1,128)} %dynamic-slice_bitcast_fusion.hb_row), custom_call_target="tpu_custom_call" | custom-call | tf_op jit(solution)/shard_map/pallas_call | solution.py:145
  202.7 0.0 copy-start
  202.7 1.0 copy-done
  (1 shorter events, 0.0 us)
Async XLA Ops:
  6.5 181.6 %reduce-scatter.5.cloned.1.call-start = ((), (), s32[]{:S(2)}) async-start(), calls=%async_computation.3 | async-start | bytes 4055040 | tf_op jit(solution)/shard_map/reduce_scatter | solution.py:140
  80.1 0.7 copy-start.1
  202.7 1.1 copy-start
Sparse Core Ops, SparseCore 0:
  80.2 107.8 reduce-scatter.4
where the time goes:
time: 211 us
  waiting for transfers between devices  104 us (49%)
  Pallas kernels  48.6 us (23%)
  local copies, waits for them, and re-layouts  30.2 us (14%)
  between operations  14.1 us (7%)
  blocking collectives  11.7 us (6%)
  other arithmetic  2.45 us (1%)
    reduce_scatter x1, waiting for transfers between devices, part(): lax.psum_scatter(partial_sums, ('wide', 'narrow'), scatter_dimension=0, t...  104 us
    pallas_call x1, Pallas kernels, part(): pl.pallas_call(functools.partial(contract, cap, wide), out_shape=jax.Shap...  45.8 us
    unnamed x5, local copies, waits for them, and re-layouts  20.8 us
    all_gather x1, blocking collectives, part(): summed = lax.all_gather(mine, 'narrow', axis=0, tiled=True)  11.7 us
  transfers between devices with their start and end apart: 1, of which 1 were waited for; matrix products, arithmetic and copies ran while one was open for 2% of the time, Pallas kernels for 0%

commit v1 on v0

v1 whole, which is shorter than its diff:
```python
import functools

import jax
import jax.numpy as jnp
from jax import lax
from jax.experimental import pallas as pl
from jax.experimental.pallas import tpu as pltpu
from jax.sharding import PartitionSpec as P

IRREPS = 8
FEWEST = 64
LANES = 128
MESH = pl.DeviceIdType.MESH


def split(x):
    high = x.astype(jnp.bfloat16)
    low = (x - high.astype(jnp.float32)).astype(jnp.bfloat16)
    return high, low


def block_starts(labels):
    return [
        jnp.sum((labels < h).astype(jnp.int32), axis=1, keepdims=True) for h in range(1, IRREPS)
    ]


def labels_at(index, starts):
    out = jnp.zeros_like(index)
    for start in starts:
        out += (index >= start).astype(jnp.int32)
    return out


def pass_labels(index, starts, cap, turn):
    label = labels_at(index, starts)
    first = jnp.zeros_like(index)
    for start in starts:
        first = jnp.where(index >= start, start, first)
    place = index - first
    return jnp.where((place >= turn * cap) & (place < (turn + 1) * cap), label, 8 * IRREPS)


def contract(cap, turn, wide, rows_w, kp, step, occ, slab, a_ref, w_ref, v_ref, out_ref, hc, lcat, lt, wcat, acc):
    k, n_k = pl.program_id(0), pl.num_programs(0)
    ni, _, nc, va = a_ref.shape
    vb = w_ref.shape[3]
    m = ni * cap
    bw = vb // wide
    starts = block_starts(v_ref[...])

    @pl.when(k == 0)
    def _():
        at = lax.axis_index("narrow") * nc + lax.broadcasted_iota(jnp.int32, (nc, LANES), 0)
        hc[...] = labels_at(at, starts)
        if kp != nc:
            lcat[...] = jnp.zeros_like(lcat)
            wcat[...] = jnp.zeros_like(wcat)

    hk = occ[lax.axis_index("wide") * n_k + k]
    own = [occ[slab[i]] ^ hk for i in range(ni)]
    lab_b = v_ref[...]
    lab_a = pass_labels(lax.broadcasted_iota(jnp.int32, (1, va), 1), starts, cap, turn)
    lane = lax.broadcasted_iota(jnp.int32, (step, m), 1)

    def build(r, _):
        at = pl.multiple_of(r * step, step)
        rows = pl.ds(at, step)
        hcr = hc[rows, :]
        kept = None
        for i in range(ni):
            g = hcr ^ own[i]
            tiles = []
            for t in range(m // LANES):
                tile = jnp.zeros((step, LANES), jnp.float32)
                for s in range(t, va // LANES, m // LANES):
                    lanes = slice(s * LANES, (s + 1) * LANES)
                    tile = jnp.where(g == lab_a[:, lanes], a_ref[i, 0, rows, lanes], tile)
                tiles.append(tile)
            x = jnp.concatenate(tiles, axis=1)
            turns = ni // 2
            while turns:
                x = x + pltpu.roll(x, turns * cap, axis=1)
                turns //= 2
            kept = x if kept is None else jnp.where(lane >= i * cap, x, kept)
        hi, lo = split(kept)
        for n, part in enumerate((hi, hi, lo)):
            lcat[pl.ds(n * kp + at, step), :] = part
        for j in range(ni):
            g = hcr ^ own[j]
            for s in range(vb // LANES):
                lanes = slice(s * LANES, (s + 1) * LANES)
                to = slice(j * vb + s * LANES, j * vb + (s + 1) * LANES)
                x = jnp.where(g == lab_b[:, lanes], w_ref[0, rows, j, lanes], 0.0)
                hi, lo = split(x)
                for n, part in enumerate((hi, lo, hi)):
                    wcat[pl.ds(n * kp + at, step), to] = part
        return 0

    lax.fori_loop(0, nc // step, build, 0)
    lt[...] = lcat[...].T
    for n in range(0, ni * vb, 4 * LANES):
        cols = slice(n, n + 4 * LANES)
        term = jnp.dot(lt[...], wcat[:, cols], preferred_element_type=jnp.float32)

        @pl.when(k == 0)
        def _():
            acc[:, cols] = term

        @pl.when(k > 0)
        def _():
            acc[:, cols] += term

    @pl.when(k == n_k - 1)
    def _():
        for j in range(ni):
            turned = acc[:, j * vb : (j + 1) * vb].T
            for w in range(wide):
                out_ref[w * rows_w + j * bw : w * rows_w + (j + 1) * bw, :] = turned[w * bw : (w + 1) * bw]
        if rows_w != ni * bw:
            for w in range(wide):
                out_ref[w * rows_w + ni * bw : (w + 1) * rows_w, :] = jnp.zeros((rows_w - ni * bw, m), jnp.float32)


def exchange(bits, groups, p_ref, out_ref, s_ref, r0, *rest):
    n_bufs = sum(len(order) for _, _, order, _ in groups) + len(groups)
    bufs, sems = list(rest[:n_bufs]), rest[n_bufs:]
    pair_s, pair_r, own_sem, half_s, half_r, z_s, z_r, grow_s, grow_r = sems
    zs = p_ref.shape[0]
    w, n = lax.axis_index("wide"), lax.axis_index("narrow")
    core, z = lax.rem(w, 2), lax.div(w, 2)
    bit = [lax.rem(lax.div(n, 1 << b), 2) for b in range(bits)]

    def at_bit(b):
        return n + (1 << b) * (1 - 2 * bit[b])

    pair = (w + 1 - 2 * core, n)
    peers = [lax.rem(z + t, zs) for t in range(1, zs)]
    near = [pair] + [(w, at_bit(b)) for b in range(bits)] + [(2 * p + core, n) for p in peers]
    barrier = pltpu.get_barrier_semaphore()
    for device in near:
        pl.semaphore_signal(barrier, inc=1, device_id=device, device_id_type=MESH)
    pl.semaphore_wait(barrier, len(near))

    half_buf, z_buf = [], []
    for _, _, order, _ in groups:
        half_buf.append([bufs.pop(0) for _ in order])
        z_buf.append(bufs.pop(0))

    def send(src, dst, s_sem, r_sem, device):
        return pltpu.make_async_remote_copy(
            src_ref=src, dst_ref=dst, send_sem=s_sem, recv_sem=r_sem, device_id=device, device_id_type=MESH
        )

    pending = []
    chunks = peers + [z]
    pairs, owns = [], []
    for t, c in enumerate(chunks):
        cp = send(p_ref.at[c, 1 - core], r0.at[t], pair_s.at[t], pair_r.at[t], pair)
        cp.start()
        own = pltpu.make_async_copy(p_ref.at[c, core], s_ref.at[t], own_sem.at[t])
        own.start()
        pairs.append(cp)
        owns.append(own)

    def spans(g):
        first, rows, order, _ = groups[g]
        start, length, out = first, rows, [(first, rows)]
        for b in order:
            length //= 2
            start = start + length * bit[b]
            out.append((start, length))
        return out

    where = [spans(g) for g in range(len(groups))]

    def ds(start, length):
        return pl.ds(pl.multiple_of(start, 8), length)

    def start_half(g, level, t):
        b = groups[g][2][level]
        first, length = where[g][level + 1]
        other = first + length * (1 - 2 * bit[b])
        cp = send(
            s_ref.at[t, ds(other, length)],
            half_buf[g][level].at[t],
            half_s.at[g, level, t],
            half_r.at[g, level, t],
            (w, at_bit(b)),
        )
        cp.start()
        pending.append(cp)
        return cp

    def take_half(g, level, t, cp):
        cp.wait_recv()
        span = ds(*where[g][level + 1])
        s_ref[t, span] += half_buf[g][level][t]

    def start_z(g, t, level):
        span = ds(*where[g][level])
        cp = send(s_ref.at[t, span], z_buf[g].at[t], z_s.at[g, t], z_r.at[g, t], (2 * chunks[t] + core, n))
        cp.start()
        pending.append(cp)
        return cp

    def take_z(g, level, copies):
        span = ds(*where[g][level])
        total = s_ref[zs - 1, span]
        for t, cp in enumerate(copies):
            cp.wait_recv()
            total = total + z_buf[g][t]
        s_ref[zs - 1, span] = total

    late = [g for g in range(len(groups)) if groups[g][3]]
    soon = [g for g in range(len(groups)) if not groups[g][3]]
    halves = {}
    zsend = {g: [] for g in range(len(groups))}
    for t in range(zs):
        pairs[t].wait_recv()
        owns[t].wait()
        s_ref[t] += r0[t]
        for g in late:
            halves[g, 0, t] = start_half(g, 0, t)
        if t < zs - 1:
            for g in soon:
                zsend[g].append(start_z(g, t, 0))
    for level in range(bits):
        for t in range(zs):
            for g in late:
                take_half(g, level, t, halves[g, level, t])
                if level + 1 < bits:
                    halves[g, level + 1, t] = start_half(g, level + 1, t)
                elif t < zs - 1:
                    zsend[g].append(start_z(g, t, bits))
    for g in soon:
        take_z(g, 0, zsend[g])
        halves[g, 0] = start_half(g, 0, zs - 1)
    for level in range(bits):
        for g in soon:
            take_half(g, level, zs - 1, halves[g, level])
            if level + 1 < bits:
                halves[g, level + 1] = start_half(g, level + 1, zs - 1)
    for g in late:
        take_z(g, bits, zsend[g])

    for g in range(len(groups)):
        span = ds(*where[g][bits])
        out_ref[span] = s_ref[zs - 1, span]
    grows = {}
    for level in reversed(range(bits)):
        for g in range(len(groups)):
            if level + 1 < bits:
                grows[g, level + 1].wait_recv()
            span = ds(*where[g][level + 1])
            b = groups[g][2][level]
            cp = send(out_ref.at[span], out_ref.at[span], grow_s.at[g, level], grow_r.at[g, level], (w, at_bit(b)))
            cp.start()
            pending.append(cp)
            grows[g, level] = cp
    for g in range(len(groups)):
        grows[g, 0].wait_recv()
    for cp in pairs + pending:
        cp.wait_send()


def unpack(cap, turn, occ, slab, g_ref, v_ref, lane_ref, out_ref, buf):
    ni, _, na, bw = out_ref.shape
    starts = block_starts(v_ref[...])
    a0 = lax.axis_index("narrow") * na
    lab_a = pass_labels(a0 + lax.broadcasted_iota(jnp.int32, (na, bw), 0), starts, cap, turn)
    b0 = lax.axis_index("wide") * bw
    lab_b = labels_at(b0 + lax.broadcasted_iota(jnp.int32, (na, bw), 1), starts)
    both = lab_a ^ lab_b
    own = [occ[slab[i]] for i in range(ni)]
    first = pl.multiple_of(lax.rem(a0, cap), 8)
    for j in range(ni):
        turned = g_ref[j * bw : (j + 1) * bw, :].T
        for i in range(ni):
            for n in range(buf.shape[0] // cap):
                buf[n * cap : (n + 1) * cap, :] = turned[i * cap : (i + 1) * cap]
            out_ref[i, j] = jnp.where(both == (own[i] ^ own[j]), buf[pl.ds(first, na), :], 0.0)


def local(amplitudes, cycle_block, occupied_irreps, virtual_irreps, slab_orbitals):
    ni, n_k, va, nc = amplitudes.shape
    vb = cycle_block.shape[3]
    wide, narrow = lax.axis_size("wide"), lax.axis_size("narrow")
    bits = narrow.bit_length() - 1
    zs = wide // 2
    bw, na = vb // wide, va // narrow
    most = va - (IRREPS - 1) * FEWEST
    cap = most // 2
    m = ni * cap
    step = 16 if nc % 16 == 0 else nc
    kp = -(-nc // 16) * 16
    unit = 8 * narrow
    units = -(-ni * bw // unit)
    rows_w = units * unit
    amps = jnp.swapaxes(amplitudes, 2, 3)
    virt = virtual_irreps[None, :]
    up, down = tuple(range(bits)), tuple(reversed(range(bits)))
    share = [-(-2 * units // 5), 0, 0]
    share[1] = min(-(-3 * units // 10), units - share[0])
    share[2] = units - share[0] - share[1]
    groups, first = [], 0
    for n, (order, last) in zip(share, ((up, True), (down, True), (up, False))):
        if n:
            groups.append((first, n * unit, order, last))
            first += n * unit

    bufs = []
    for _, rows, order, last in groups:
        for level in range(bits):
            bufs.append(pltpu.VMEM((zs, rows >> (level + 1), m), jnp.float32))
        bufs.append(pltpu.VMEM((zs, rows >> bits if last else rows, m), jnp.float32))
    dma = pltpu.SemaphoreType.DMA
    ng = len(groups)

    def part(turn):
        partial_sums = pl.pallas_call(
            functools.partial(contract, cap, turn, wide, rows_w, kp, step),
            out_shape=jax.ShapeDtypeStruct((wide * rows_w, m), jnp.float32),
            grid_spec=pltpu.PrefetchScalarGridSpec(
                num_scalar_prefetch=2,
                grid=(n_k,),
                in_specs=[
                    pl.BlockSpec((ni, 1, nc, va), lambda k, *_: (0, k, 0, 0)),
                    pl.BlockSpec((1, nc, ni, vb), lambda k, *_: (k, 0, 0, 0)),
                    pl.BlockSpec((1, va), lambda k, *_: (0, 0)),
                ],
                out_specs=pl.BlockSpec((wide * rows_w, m), lambda k, *_: (0, 0)),
                scratch_shapes=[
                    pltpu.VMEM((nc, LANES), jnp.int32),
                    pltpu.VMEM((3 * kp, m), jnp.bfloat16),
                    pltpu.VMEM((m, 3 * kp), jnp.bfloat16),
                    pltpu.VMEM((3 * kp, ni * vb), jnp.bfloat16),
                    pltpu.VMEM((m, ni * vb), jnp.float32),
                ],
            ),
            compiler_params=pltpu.CompilerParams(vmem_limit_bytes=60 * 2**20),
            name="contract",
        )(occupied_irreps, slab_orbitals, amps, cycle_block, virt)
        summed = pl.pallas_call(
            functools.partial(exchange, bits, groups),
            out_shape=jax.ShapeDtypeStruct((rows_w, m), jnp.float32),
            in_specs=[pl.BlockSpec(memory_space=pl.ANY)],
            out_specs=pl.BlockSpec(memory_space=pltpu.VMEM),
            scratch_shapes=[
                pltpu.VMEM((zs, rows_w, m), jnp.float32),
                pltpu.VMEM((zs, rows_w, m), jnp.float32),
                *bufs,
                dma((zs,)),
                dma((zs,)),
                dma((zs,)),
                dma((ng, bits, zs)),
                dma((ng, bits, zs)),
                dma((ng, zs)),
                dma((ng, zs)),
                dma((ng, bits)),
                dma((ng, bits)),
            ],
            compiler_params=pltpu.CompilerParams(
                collective_id=turn, has_side_effects=True, vmem_limit_bytes=40 * 2**20
            ),
            name="exchange",
        )(partial_sums.reshape(zs, 2, rows_w, m))
        return pl.pallas_call(
            functools.partial(unpack, cap, turn),
            out_shape=jax.ShapeDtypeStruct((ni, ni, na, bw), jnp.float32),
            grid_spec=pltpu.PrefetchScalarGridSpec(
                num_scalar_prefetch=2,
                grid=(1,),
                in_specs=[
                    pl.BlockSpec((rows_w, m), lambda k, *_: (0, 0)),
                    pl.BlockSpec((1, va), lambda k, *_: (0, 0)),
                    pl.BlockSpec((1, va), lambda k, *_: (0, 0)),
                ],
                out_specs=pl.BlockSpec((ni, ni, na, bw), lambda k, *_: (0, 0, 0, 0)),
                scratch_shapes=[pltpu.VMEM(((-(-na // cap) + 1) * cap, bw), jnp.float32)],
            ),
            name="unpack",
        )(occupied_irreps, slab_orbitals, summed, virt, virt)

    names = jnp.arange(IRREPS, dtype=jnp.int32)
    longest = jnp.max(jnp.sum((virtual_irreps[None, :] == names[:, None]).astype(jnp.int32), axis=1))
    return lax.cond(longest > cap, lambda x: x + part(1), lambda x: x, part(0))


def solution(mesh):
    placed = (P(None, "wide", None, "narrow"), P("wide", "narrow", None, None), P(), P(), P())
    return jax.shard_map(
        local,
        mesh=mesh,
        in_specs=placed,
        out_specs=P(None, None, "narrow", "wide"),
        check_vma=False,
    )
```

time: 211 us -> 91.6 us (0.43)
  the two profiles are of different devices: /device:TPU:0 before, /device:TPU:12 now
where the time goes in v1:
time: 91.6 us; the launch traced here: 91.3 us
  Pallas kernels  84.5 us (92%)
  local copies, waits for them, and re-layouts  4.66 us (5%)
  other arithmetic  1.44 us (2%)
    pallas_call x1, Pallas kernels, part(): pl.pallas_call(functools.partial(contract, cap, turn, wide, rows_w, kp, s...  44.2 us
    pallas_call x1, Pallas kernels, part(): pl.pallas_call(functools.partial(exchange, bits, groups), out_shape=jax.S...  38.1 us
    unnamed x10, local copies, waits for them, and re-layouts  3.97 us
    pallas_call x1, Pallas kernels, part(): pl.pallas_call(functools.partial(unpack, cap, turn), out_shape=jax.ShapeD...  2.26 us

profile of v1, /device:TPU:12, one launch (start us, length us, event | category | flops | bytes accessed | tf_op | source)
XLA Modules:
  0.0 91.3 jit_solution(16676884149593962954)
XLA Ops:
  0.0 0.8 convert_reduce_fusion
  0.8 0.6 reduce_max.9
  2.1 0.7 broadcast_in_dim.2.v_ref.lane_ref
  2.8 44.2 %contract.3 = f32[2560,384]{1,0:T(8,128)} custom-call(s32[64]{0:T(128)} %occ.3, s32[4]{0:T(128)} %slab.3, f32[4,8,160,640]{3,2,1,0:T(8,128)} %bitcast.5, f32[8,160,4,640]{3,2,1,0:T(4,128)} %w_ref.1, s32[1,640]{1,0:T(1,128)S(1)} %broadcast_in_dim.2.v_ref.lane_ref), custom_call_target="tpu_custom_call" | custom-call | tf_op jit(solution)/shard_map/contract/pallas_call | solution.py:321
  46.9 0.0 copy-start.5
  46.9 0.0 copy-start.6
  47.0 0.0 copy-start
  47.0 2.1 %copy-done = f32[2560,384]{1,0:T(8,128)S(1)} copy-done((f32[2560,384]{1,0:T(8,128)S(1)}, f32[2560,384]{1,0:T(8,128)}, u32[]{:S(2)}) %copy-start) | copy-done | bytes 3932184
  49.1 38.1 %exchange.3.g_ref = f32[320,384]{1,0:T(8,128)S(1)} custom-call(f32[4,2,320,384]{3,2,1,0:T(8,128)S(1)} %bitcast.3), custom_call_target="tpu_custom_call" | custom-call | tf_op jit(solution)/shard_map/exchange/pallas_call | solution.py:344
  87.2 0.0 copy-start.2
  87.2 0.8 copy-done.2
  88.0 0.0 copy-done.5
  88.0 0.0 copy-done.6
  88.0 2.3 %unpack.3 = f32[4,4,160,80]{3,2,1,0:T(8,128)S(1)} custom-call(s32[64]{0:T(128)S(1)} %copy-done.5, s32[4]{0:T(128)S(1)} %copy-done.6, f32[320,384]{1,0:T(8,128)} %copy-done.2, s32[1,640]{1,0:T(1,128)S(1)} %broadcast_in_dim.2.v_ref.lane_ref, s32[1,640]{1,0:T(1,128)S(1)} %broadcast_in_dim.2.v_ref.lane_ref), custom_call_target="tpu_custom_call" | custom-call | tf_op jit(solution)/shard_map/unpack/pallas_call | solution.py:368
  90.3 0.0 copy-start.4
  90.3 1.0 %copy-done.4 = f32[4,4,160,80]{3,2,1,0:T(8,128)} copy-done((f32[4,4,160,80]{3,2,1,0:T(8,128)}, f32[4,4,160,80]{3,2,1,0:T(8,128)S(1)}, u32[]{:S(2)}) %copy-start.4) | copy-done | bytes 819224
  (1 shorter events, 0.0 us)
Async XLA Ops:
  46.9 41.0 %copy-start.5 = (s32[64]{0:T(128)S(1)}, s32[64]{0:T(128)}, u32[]{:S(2)}) copy-start(s32[64]{0:T(128)} %occ.3) | copy-start | bytes 772
  46.9 41.0 %copy-start.6 = (s32[4]{0:T(128)S(1)}, s32[4]{0:T(128)}, u32[]{:S(2)}) copy-start(s32[4]{0:T(128)} %slab.3) | copy-start | bytes 52
  47.0 2.1 %copy-start = (f32[2560,384]{1,0:T(8,128)S(1)}, f32[2560,384]{1,0:T(8,128)}, u32[]{:S(2)}) copy-start(f32[2560,384]{1,0:T(8,128)} %contract.3) | copy-start | bytes 11796484
  87.2 0.8 copy-start.2
  90.3 1.1 %copy-start.4 = (f32[4,4,160,80]{3,2,1,0:T(8,128)}, f32[4,4,160,80]{3,2,1,0:T(8,128)S(1)}, u32[]{:S(2)}) copy-start(f32[4,4,160,80]{3,2,1,0:T(8,128)S(1)} %get-tuple-element.30) | copy-start | bytes 2457604

commit v2 on v1

--- a/solution.py
+++ b/solution.py
@@ -41,16 +41,36 @@
     return jnp.where((place >= turn * cap) & (place < (turn + 1) * cap), label, 8 * IRREPS)
 
 
-def contract(cap, turn, wide, rows_w, kp, step, occ, slab, a_ref, w_ref, v_ref, out_ref, hc, lcat, lt, wcat, acc):
+def contract(cap, turn, wide, rows_w, kp, step, occ, slab, a_ref, w_ref, v_ref, out_ref, hc, lcat, lt, wcat, acc, tbuf, wbuf, labs, t_sem, w_sem):
     k, n_k = pl.program_id(0), pl.num_programs(0)
     ni, _, nc, va = a_ref.shape
     vb = w_ref.shape[3]
     m = ni * cap
     bw = vb // wide
-    starts = block_starts(v_ref[...])
+
+    def fetch(at, slot):
+        return [pltpu.make_async_copy(a_ref.at[:, at], tbuf.at[slot], t_sem.at[slot])] + [
+            pltpu.make_async_copy(w_ref.at[at, :, j, :], wbuf.at[slot, j], w_sem.at[slot, j]) for j in range(ni)
+        ]
+
+    slot = lax.rem(k, 2)
 
     @pl.when(k == 0)
     def _():
+        for copy in fetch(0, 0):
+            copy.start()
+
+    @pl.when(k + 1 < n_k)
+    def _():
+        for copy in fetch(k + 1, 1 - slot):
+            copy.start()
+
+    @pl.when(k == 0)
+    def _():
+        acc[...] = jnp.zeros_like(acc)
+        starts = block_starts(v_ref[...])
+        labs[:8, :] = jnp.broadcast_to(pass_labels(lax.broadcasted_iota(jnp.int32, (8, va), 1), starts, cap, turn), (8, va))
+        labs[8:, :] = jnp.broadcast_to(v_ref[...], (8, va))
         at = lax.axis_index("narrow") * nc + lax.broadcasted_iota(jnp.int32, (nc, LANES), 0)
         hc[...] = labels_at(at, starts)
         if kp != nc:
@@ -59,14 +79,14 @@
 
     hk = occ[lax.axis_index("wide") * n_k + k]
     own = [occ[slab[i]] ^ hk for i in range(ni)]
-    lab_b = v_ref[...]
-    lab_a = pass_labels(lax.broadcasted_iota(jnp.int32, (1, va), 1), starts, cap, turn)
     lane = lax.broadcasted_iota(jnp.int32, (step, m), 1)
+    for copy in fetch(k, slot):
+        copy.wait()
 
     def build(r, _):
         at = pl.multiple_of(r * step, step)
         rows = pl.ds(at, step)
-        hcr = hc[rows, :]
+        hcr = hc[rows, :].reshape(step // 8, 8, LANES)
         kept = None
         for i in range(ni):
             g = hcr ^ own[i]
@@ -75,7 +95,8 @@
                 tile = jnp.zeros((step, LANES), jnp.float32)
                 for s in range(t, va // LANES, m // LANES):
                     lanes = slice(s * LANES, (s + 1) * LANES)
-                    tile = jnp.where(g == lab_a[:, lanes], a_ref[i, 0, rows, lanes], tile)
+                    mask = (g == labs[:8, lanes][None]).reshape(step, LANES)
+                    tile = jnp.where(mask, tbuf[slot, i, rows, lanes], tile)
                 tiles.append(tile)
             x = jnp.concatenate(tiles, axis=1)
             turns = ni // 2
@@ -91,7 +112,8 @@
             for s in range(vb // LANES):
                 lanes = slice(s * LANES, (s + 1) * LANES)
                 to = slice(j * vb + s * LANES, j * vb + (s + 1) * LANES)
-                x = jnp.where(g == lab_b[:, lanes], w_ref[0, rows, j, lanes], 0.0)
+                mask = (g == labs[8:, lanes][None]).reshape(step, LANES)
+                x = jnp.where(mask, wbuf[slot, j, rows, lanes], 0.0)
                 hi, lo = split(x)
                 for n, part in enumerate((hi, lo, hi)):
                     wcat[pl.ds(n * kp + at, step), to] = part
@@ -101,15 +123,7 @@
     lt[...] = lcat[...].T
     for n in range(0, ni * vb, 4 * LANES):
         cols = slice(n, n + 4 * LANES)
-        term = jnp.dot(lt[...], wcat[:, cols], preferred_element_type=jnp.float32)
-
-        @pl.when(k == 0)
-        def _():
-            acc[:, cols] = term
-
-        @pl.when(k > 0)
-        def _():
-            acc[:, cols] += term
+        acc[:, cols] += jnp.dot(lt[...], wcat[:, cols], preferred_element_type=jnp.float32)
 
     @pl.when(k == n_k - 1)
     def _():
@@ -292,7 +306,7 @@
     most = va - (IRREPS - 1) * FEWEST
     cap = most // 2
     m = ni * cap
-    step = 16 if nc % 16 == 0 else nc
+    step = 32 if nc % 32 == 0 else nc
     kp = -(-nc // 16) * 16
     unit = 8 * narrow
     units = -(-ni * bw // unit)
@@ -325,8 +339,8 @@
                 num_scalar_prefetch=2,
                 grid=(n_k,),
                 in_specs=[
-                    pl.BlockSpec((ni, 1, nc, va), lambda k, *_: (0, k, 0, 0)),
-                    pl.BlockSpec((1, nc, ni, vb), lambda k, *_: (k, 0, 0, 0)),
+                    pl.BlockSpec(memory_space=pltpu.HBM),
+                    pl.BlockSpec(memory_space=pltpu.HBM),
                     pl.BlockSpec((1, va), lambda k, *_: (0, 0)),
                 ],
                 out_specs=pl.BlockSpec((wide * rows_w, m), lambda k, *_: (0, 0)),
@@ -336,9 +350,14 @@
                     pltpu.VMEM((m, 3 * kp), jnp.bfloat16),
                     pltpu.VMEM((3 * kp, ni * vb), jnp.bfloat16),
                     pltpu.VMEM((m, ni * vb), jnp.float32),
+                    pltpu.VMEM((2, ni, nc, va), jnp.float32),
+                    pltpu.VMEM((2, ni, nc, vb), jnp.float32),
+                    pltpu.VMEM((16, va), jnp.int32),
+                    dma((2,)),
+                    dma((2, ni)),
                 ],
             ),
-            compiler_params=pltpu.CompilerParams(vmem_limit_bytes=60 * 2**20),
+            compiler_params=pltpu.CompilerParams(vmem_limit_bytes=54 * 2**20),
             name="contract",
         )(occupied_irreps, slab_orbitals, amps, cycle_block, virt)
         summed = pl.pallas_call(
@@ -361,7 +380,7 @@
                 dma((ng, bits)),
             ],
             compiler_params=pltpu.CompilerParams(
-                collective_id=turn, has_side_effects=True, vmem_limit_bytes=40 * 2**20
+                collective_id=turn, has_side_effects=True, vmem_limit_bytes=54 * 2**20
             ),
             name="exchange",
         )(partial_sums.reshape(zs, 2, rows_w, m))
@@ -379,6 +398,7 @@
                 out_specs=pl.BlockSpec((ni, ni, na, bw), lambda k, *_: (0, 0, 0, 0)),
                 scratch_shapes=[pltpu.VMEM(((-(-na // cap) + 1) * cap, bw), jnp.float32)],
             ),
+            compiler_params=pltpu.CompilerParams(vmem_limit_bytes=54 * 2**20),
             name="unpack",
         )(occupied_irreps, slab_orbitals, summed, virt, virt)
 

time: 91.6 us -> 72.4 us (0.79)
  Pallas kernels: 84.5 us -> 68.2 us
  local copies, waits for them, and re-layouts: 4.66 us -> 1.76 us
    pallas_call x1, Pallas kernels: 44.2 us -> 26.8 us  [part(): pl.pallas_call(functools.partial(contract, cap, turn, wide, rows_w, kp, s...]
    unnamed x10 -> x6, local copies, waits for them, and re-layouts: 3.97 us -> 1.06 us
    pallas_call x1, Pallas kernels: 38.1 us -> 39.2 us  [part(): pl.pallas_call(functools.partial(exchange, bits, groups), out_shape=jax.S...]
where the time goes in v2:
time: 72.4 us; the launch traced here: 72.2 us
  Pallas kernels  68.2 us (94%)
  local copies, waits for them, and re-layouts  1.76 us (2%)
  other arithmetic  1.44 us (2%)
  between operations  0.73 us (1%)
    pallas_call x1, Pallas kernels, part(): pl.pallas_call(functools.partial(exchange, bits, groups), out_shape=jax.S...  39.2 us
    pallas_call x1, Pallas kernels, part(): pl.pallas_call(functools.partial(contract, cap, turn, wide, rows_w, kp, s...  26.8 us
    pallas_call x1, Pallas kernels, part(): pl.pallas_call(functools.partial(unpack, cap, turn), out_shape=jax.ShapeD...  2.27 us

profile of v2, /device:TPU:12, one launch (start us, length us, event | category | flops | bytes accessed | tf_op | source)
XLA Modules:
  0.0 72.2 jit_solution(9367159270725266929)
XLA Ops:
  0.0 0.8 %convert_reduce_fusion = s32[8]{0:T(128)S(1)} fusion(s32[640]{0:T(1024)} %param.10), kind=kLoop, calls=%fused_computation | loop fusion | flops 15352 | bytes 2592 | tf_op jit(solution)/shard_map/reduce_sum | solution.py:406
  0.8 0.6 reduce_max.9
  2.1 0.7 broadcast_in_dim.2.v_ref.lane_ref
  2.8 26.8 %contract.3 = f32[2560,384]{1,0:T(8,128)} custom-call(s32[64]{0:T(128)} %occ.3, s32[4]{0:T(128)} %slab.3, f32[4,8,160,640]{3,2,1,0:T(8,128)} %bitcast.3, f32[8,160,4,640]{3,2,1,0:T(4,128)} %w_ref.1, s32[1,640]{1,0:T(1,128)S(1)} %broadcast_in_dim.2.v_ref.lane_ref), custom_call_target="tpu_custom_call" | custom-call | tf_op jit(solution)/shard_map/contract/pallas_call | solution.py:335
  29.6 0.0 copy-start.1
  29.6 0.0 copy-start.2
  29.6 39.2 %exchange.3.g_ref = f32[320,384]{1,0:T(8,128)} custom-call(f32[4,2,320,384]{3,2,1,0:T(8,128)} %bitcast.5), custom_call_target="tpu_custom_call" | custom-call | tf_op jit(solution)/shard_map/exchange/pallas_call | solution.py:363
  68.8 0.0 copy-done.1
  68.8 0.0 copy-done.2
  68.8 2.3 %unpack.3 = f32[4,4,160,80]{3,2,1,0:T(8,128)S(1)} custom-call(s32[64]{0:T(128)S(1)} %copy-done.1, s32[4]{0:T(128)S(1)} %copy-done.2, f32[320,384]{1,0:T(8,128)} %exchange.3.g_ref, s32[1,640]{1,0:T(1,128)S(1)} %broadcast_in_dim.2.v_ref.lane_ref, s32[1,640]{1,0:T(1,128)S(1)} %broadcast_in_dim.2.v_ref.lane_ref), custom_call_target="tpu_custom_call" | custom-call | tf_op jit(solution)/shard_map/unpack/pallas_call | solution.py:387
  71.1 0.0 copy-start
  71.1 1.0 %copy-done = f32[4,4,160,80]{3,2,1,0:T(8,128)} copy-done((f32[4,4,160,80]{3,2,1,0:T(8,128)}, f32[4,4,160,80]{3,2,1,0:T(8,128)S(1)}, u32[]{:S(2)}) %copy-start) | copy-done | bytes 819224
  (1 shorter events, 0.0 us)
Async XLA Ops:
  29.6 39.2 %copy-start.1 = (s32[64]{0:T(128)S(1)}, s32[64]{0:T(128)}, u32[]{:S(2)}) copy-start(s32[64]{0:T(128)} %occ.3) | copy-start | bytes 772
  29.6 39.2 %copy-start.2 = (s32[4]{0:T(128)S(1)}, s32[4]{0:T(128)}, u32[]{:S(2)}) copy-start(s32[4]{0:T(128)} %slab.3) | copy-start | bytes 52
  71.1 1.1 %copy-start = (f32[4,4,160,80]{3,2,1,0:T(8,128)}, f32[4,4,160,80]{3,2,1,0:T(8,128)S(1)}, u32[]{:S(2)}) copy-start(f32[4,4,160,80]{3,2,1,0:T(8,128)S(1)} %get-tuple-element.30) | copy-start | bytes 2457604

commit v3 on v0

v3 whole, which is shorter than its diff:
```python
import functools

import jax
import jax.numpy as jnp
from jax import lax
from jax.experimental import pallas as pl
from jax.experimental.pallas import tpu as pltpu
from jax.sharding import PartitionSpec as P

IRREPS = 8
FEWEST = 64
LANES = 128
MESH = pl.DeviceIdType.MESH


def split(x):
    high = x.astype(jnp.bfloat16)
    low = (x - high.astype(jnp.float32)).astype(jnp.bfloat16)
    return high, low


def block_starts(labels):
    out = []
    for h in range(1, IRREPS):
        below = jnp.sum((labels < h).astype(jnp.int32), axis=1, keepdims=True)
        out.append(jnp.sum(below, axis=0, keepdims=True))
    return out


def labels_at(index, starts):
    out = jnp.zeros_like(index)
    for start in starts:
        out += (index >= start).astype(jnp.int32)
    return out


def pass_labels(index, starts, cap, turn):
    label = labels_at(index, starts)
    first = jnp.zeros_like(index)
    for start in starts:
        first = jnp.where(index >= start, start, first)
    place = index - first
    return jnp.where((place >= turn * cap) & (place < (turn + 1) * cap), label, 8 * IRREPS)


def fused(cap, turn, kp, step, bits, groups, segments, occ, slab, a_ref, w_ref, v_ref, out_ref, *rest):
    n_bufs = sum(len(order) for _, _, order, _ in groups) + len(groups)
    (hc, lcat, lt, wcat, acc, tbuf, wbuf, labs, sums, s_ref, r0), rest = rest[:11], list(rest[11:])
    bufs, sems = rest[:n_bufs], rest[n_bufs:]
    t_sem, w_sem, pair_s, pair_r, half_s, half_r, z_s, z_r, grow_s, grow_r = sems
    ni, n_k, nc, va = a_ref.shape
    vb = w_ref.shape[3]
    turns_j, zs, _, rows_c, m = sums.shape
    nj = ni // turns_j
    bw = vb // (2 * zs)
    w, n = lax.axis_index("wide"), lax.axis_index("narrow")
    core, z = lax.rem(w, 2), lax.div(w, 2)
    bit = [lax.rem(lax.div(n, 1 << b), 2) for b in range(bits)]

    def at_bit(b):
        return n + (1 << b) * (1 - 2 * bit[b])

    pair = (w + 1 - 2 * core, n)
    peers = [lax.rem(z + t, zs) for t in range(1, zs)]
    near = [pair] + [(w, at_bit(b)) for b in range(bits)] + [(2 * p + core, n) for p in peers]
    barrier = pltpu.get_barrier_semaphore()
    for device in near:
        pl.semaphore_signal(barrier, inc=1, device_id=device, device_id_type=MESH)

    def fetch_a(k, slot):
        return pltpu.make_async_copy(a_ref.at[:, k], tbuf.at[slot], t_sem.at[slot])

    def fetch_w(k, turn_j, slot):
        return [
            pltpu.make_async_copy(w_ref.at[k, :, turn_j * nj + j, :], wbuf.at[slot, j], w_sem.at[slot, j])
            for j in range(nj)
        ]

    fetch_a(0, 0).start()
    for copy in fetch_w(0, 0, 0):
        copy.start()
    starts = block_starts(v_ref[...])
    index = LANES * lax.broadcasted_iota(jnp.int32, (va // LANES, LANES), 0)
    index += lax.broadcasted_iota(jnp.int32, (va // LANES, LANES), 1)
    lab_a = pass_labels(index, starts, cap, turn)
    lab_b = v_ref[...]
    for s in range(va // LANES):
        labs[0, s] = jnp.broadcast_to(lab_a[s : s + 1], (8, LANES))
        labs[1, s] = jnp.broadcast_to(lab_b[s : s + 1], (8, LANES))
    hc[...] = labels_at(n * nc + lax.broadcasted_iota(jnp.int32, (nc, LANES), 0), starts)
    if kp != nc:
        lcat[...] = jnp.zeros_like(lcat)
        wcat[...] = jnp.zeros_like(wcat)
    if rows_c != nj * bw:
        sums[...] = jnp.zeros_like(sums)
    slab_labels = [occ[slab[i]] for i in range(ni)]

    def build_a(own, slot, r):
        lane = lax.broadcasted_iota(jnp.int32, (step, m), 1)
        at = pl.multiple_of(r * step, step)
        rows = pl.ds(at, step)
        hcr = hc[rows, :].reshape(step // 8, 8, LANES)
        kept = None
        for i in range(ni):
            g = hcr ^ own[i]
            tiles = []
            for t in range(m // LANES):
                tile = jnp.zeros((step, LANES), jnp.float32)
                for s in range(t, va // LANES, m // LANES):
                    mask = (g == labs[0, s][None]).reshape(step, LANES)
                    tile = jnp.where(mask, tbuf[slot, i, rows, s * LANES : (s + 1) * LANES], tile)
                tiles.append(tile)
            x = jnp.concatenate(tiles, axis=1)
            turns = ni // 2
            while turns:
                x = x + pltpu.roll(x, turns * cap, axis=1)
                turns //= 2
            kept = x if kept is None else jnp.where(lane >= i * cap, x, kept)
        hi, lo = split(kept)
        for p, part in enumerate((hi, hi, lo)):
            lcat[pl.ds(p * kp + at, step), :] = part

    def build_w(own, slot, r):
        at = pl.multiple_of(r * step, step)
        rows = pl.ds(at, step)
        hcr = hc[rows, :].reshape(step // 8, 8, LANES)
        for j in range(nj):
            g = hcr ^ own[j]
            for s in range(vb // LANES):
                to = slice(j * vb + s * LANES, j * vb + (s + 1) * LANES)
                mask = (g == labs[1, s][None]).reshape(step, LANES)
                x = jnp.where(mask, wbuf[slot, j, rows, s * LANES : (s + 1) * LANES], 0.0)
                hi, lo = split(x)
                for p, part in enumerate((hi, lo, hi)):
                    wcat[pl.ds(p * kp + at, step), to] = part

    def one_k(k, turn_j):
        slot = lax.rem(k + turn_j * n_k, 2)

        @pl.when(k + 1 < n_k)
        def _():
            if turn_j == 0:
                fetch_a(k + 1, 1 - slot).start()
            for copy in fetch_w(k + 1, turn_j, 1 - slot):
                copy.start()

        if turn_j + 1 < turns_j:

            @pl.when(k + 1 == n_k)
            def _():
                for copy in fetch_w(0, turn_j + 1, 1 - slot):
                    copy.start()

        hk = occ[w * n_k + k]
        own = [label ^ hk for label in slab_labels]
        if turn_j == 0:
            fetch_a(k, slot).wait()
        for copy in fetch_w(k, turn_j, slot):
            copy.wait()

        def rows_of(r, _):
            if turn_j == 0:
                build_a(own, slot, r)
            build_w(own[turn_j * nj : (turn_j + 1) * nj], slot, r)
            return 0

        lax.fori_loop(0, nc // step, rows_of, 0)
        if turn_j == 0:
            lt[k] = lcat[...].T
        for c in range(0, nj * vb, 2 * LANES):
            cols = slice(c, c + 2 * LANES)
            acc[:, cols] += jnp.dot(lt[k], wcat[:, cols], preferred_element_type=jnp.float32)

    def some_k(first, last, turn_j):
        lax.fori_loop(first, last, lambda k, _: (one_k(k, turn_j), 0)[1], 0)

    def hand_over(turn_j):
        for j in range(nj):
            turned = acc[:, j * vb : (j + 1) * vb].T
            for v in range(2 * zs):
                sums[turn_j, v // 2, v % 2, j * bw : (j + 1) * bw, :] = turned[v * bw : (v + 1) * bw]

    half_buf, z_buf = [], []
    for _, _, order, _ in groups:
        half_buf.append([bufs.pop(0) for _ in order])
        z_buf.append(bufs.pop(0))

    def spans(g):
        start, length, order, _ = groups[g]
        out = [(start, length)]
        for b in order:
            length //= 2
            start = start + length * bit[b]
            out.append((start, length))
        return out

    where = [spans(g) for g in range(len(groups))]

    def ds(start, length):
        return pl.ds(pl.multiple_of(start, 8), length)

    pending = []

    def send(src, dst, s_sem, r_sem, device):
        copy = pltpu.make_async_remote_copy(
            src_ref=src, dst_ref=dst, send_sem=s_sem, recv_sem=r_sem, device_id=device, device_id_type=MESH
        )
        copy.start()
        pending.append(copy)
        return copy

    def travel(q):
        chunks = peers + [z]
        late = [g for g in range(len(groups)) if groups[g][3]]
        soon = [g for g in range(len(groups)) if not groups[g][3]]
        own = zs - 1

        def start_half(g, level, t):
            b = groups[g][2][level]
            first, length = where[g][level + 1]
            other = first + length * (1 - 2 * bit[b])
            return send(
                s_ref.at[q, t, ds(other, length)],
                half_buf[g][level].at[q, t],
                half_s.at[q, g, level, t],
                half_r.at[q, g, level, t],
                (w, at_bit(b)),
            )

        def take_half(g, level, t, copy):
            copy.wait_recv()
            span = ds(*where[g][level + 1])
            s_ref[q, t, span] += half_buf[g][level][q, t]

        def start_z(g, t, level):
            return send(
                s_ref.at[q, t, ds(*where[g][level])],
                z_buf[g].at[q, t],
                z_s.at[q, g, t],
                z_r.at[q, g, t],
                (2 * chunks[t] + core, n),
            )

        def take_z(g, level, copies):
            span = ds(*where[g][level])
            total = s_ref[q, own, span]
            for t, copy in enumerate(copies):
                copy.wait_recv()
                total = total + z_buf[g][q, t]
            s_ref[q, own, span] = total

        def start_grow(g, level):
            span = ds(*where[g][level + 1])
            b = groups[g][2][level]
            return send(
                out_ref.at[q, span], out_ref.at[q, span], grow_s.at[q, g, level], grow_r.at[q, g, level], (w, at_bit(b))
            )

        pairs = [
            send(sums.at[q, c, 1 - core], r0.at[q, t], pair_s.at[q, t], pair_r.at[q, t], pair)
            for t, c in enumerate(chunks)
        ]
        yield
        halves, zsend = {}, {g: [] for g in range(len(groups))}
        for t, c in enumerate(chunks):
            pairs[t].wait_recv()
            s_ref[q, t] = sums[q, c, core] + r0[q, t]
            for g in late:
                halves[g, 0, t] = start_half(g, 0, t)
            if t < own:
                for g in soon:
                    zsend[g].append(start_z(g, t, 0))
        yield
        for level in range(bits):
            for t in range(zs):
                for g in late:
                    take_half(g, level, t, halves[g, level, t])
                    if level + 1 < bits:
                        halves[g, level + 1, t] = start_half(g, level + 1, t)
                    elif t < own:
                        zsend[g].append(start_z(g, t, bits))
            yield
        for g in soon:
            take_z(g, 0, zsend[g])
            halves[g, 0] = start_half(g, 0, own)
        yield
        for level in range(bits):
            for g in soon:
                take_half(g, level, own, halves[g, level])
                if level + 1 < bits:
                    halves[g, level + 1] = start_half(g, level + 1, own)
        for g in late:
            take_z(g, bits, zsend[g])
        grows = {}
        for level in reversed(range(bits)):
            for g in range(len(groups)):
                if level + 1 < bits:
                    grows[g, level + 1].wait_recv()
                else:
                    span = ds(*where[g][bits])
                    out_ref[q, span] = s_ref[q, own, span]
                grows[g, level] = start_grow(g, level)
            yield
        for g in range(len(groups)):
            grows[g, 0].wait_recv()

    acc[...] = jnp.zeros_like(acc)
    some_k(0, n_k, 0)
    hand_over(0)
    pl.semaphore_wait(barrier, len(near))
    trips = [travel(0)]
    next(trips[0])
    for q in range(1, turns_j):
        acc[...] = jnp.zeros_like(acc)
        for at in range(segments):
            some_k(at * n_k // segments, (at + 1) * n_k // segments, q)
            if at + 1 < segments:
                next(trips[0], None)
        hand_over(q)
        trips.append(travel(q))
        next(trips[q])
    while trips:
        trips = [trip for trip in trips if next(trip, "over") is None]
    for copy in pending:
        copy.wait_send()


def unpack(cap, turn, nj, occ, slab, g_ref, v_ref, out_ref, buf):
    ni, _, na, bw = out_ref.shape
    starts = block_starts(v_ref[...])
    a0 = lax.axis_index("narrow") * na
    lab_a = pass_labels(a0 + lax.broadcasted_iota(jnp.int32, (na, bw), 0), starts, cap, turn)
    b0 = lax.axis_index("wide") * bw
    lab_b = labels_at(b0 + lax.broadcasted_iota(jnp.int32, (na, bw), 1), starts)
    both = lab_a ^ lab_b
    own = [occ[slab[i]] for i in range(ni)]
    first = pl.multiple_of(lax.rem(a0, cap), 8)
    for j in range(ni):
        at = j % nj * bw
        turned = g_ref[j // nj, at : at + bw, :].T
        for i in range(ni):
            for n in range(buf.shape[0] // cap):
                buf[n * cap : (n + 1) * cap, :] = turned[i * cap : (i + 1) * cap]
            out_ref[i, j] = jnp.where(both == (own[i] ^ own[j]), buf[pl.ds(first, na), :], 0.0)


def local(amplitudes, cycle_block, occupied_irreps, virtual_irreps, slab_orbitals):
    ni, n_k, va, nc = amplitudes.shape
    vb = cycle_block.shape[3]
    wide, narrow = lax.axis_size("wide"), lax.axis_size("narrow")
    bits = narrow.bit_length() - 1
    zs = wide // 2
    bw, na = vb // wide, va // narrow
    most = va - (IRREPS - 1) * FEWEST
    cap = most // 2
    m = ni * cap
    step = 32 if nc % 32 == 0 else nc
    kp = -(-nc // 16) * 16
    unit = 8 * narrow
    turns_j = 2
    nj = ni // turns_j
    units = -(-nj * bw // unit)
    rows_c = units * unit
    amps = jnp.swapaxes(amplitudes, 2, 3)
    virt = virtual_irreps.reshape(va // LANES, LANES)
    up, down = tuple(range(bits)), tuple(reversed(range(bits)))
    share = [-(-2 * units // 5), 0, 0]
    share[1] = min(share[0], units - share[0])
    share[2] = units - share[0] - share[1]
    groups, first = [], 0
    for n, (order, last) in zip(share, ((up, True), (down, True), (up, False))):
        if n:
            groups.append((first, n * unit, order, last))
            first += n * unit

    bufs = []
    for _, rows, order, last in groups:
        for level in range(bits):
            bufs.append(pltpu.VMEM((turns_j, zs, rows >> (level + 1), m), jnp.float32))
        bufs.append(pltpu.VMEM((turns_j, zs, rows >> bits if last else rows, m), jnp.float32))
    dma = pltpu.SemaphoreType.DMA
    ng = len(groups)

    def part(turn):
        summed = pl.pallas_call(
            functools.partial(fused, cap, turn, kp, step, bits, groups, 4),
            out_shape=jax.ShapeDtypeStruct((turns_j, rows_c, m), jnp.float32),
            in_specs=[
                pl.BlockSpec(memory_space=pltpu.SMEM),
                pl.BlockSpec(memory_space=pltpu.SMEM),
                pl.BlockSpec(memory_space=pltpu.HBM),
                pl.BlockSpec(memory_space=pltpu.HBM),
                pl.BlockSpec(memory_space=pltpu.VMEM),
            ],
            out_specs=pl.BlockSpec(memory_space=pltpu.VMEM),
            scratch_shapes=[
                pltpu.VMEM((nc, LANES), jnp.int32),
                pltpu.VMEM((3 * kp, m), jnp.bfloat16),
                pltpu.VMEM((n_k, m, 3 * kp), jnp.bfloat16),
                pltpu.VMEM((3 * kp, nj * vb), jnp.bfloat16),
                pltpu.VMEM((m, nj * vb), jnp.float32),
                pltpu.VMEM((2, ni, nc, va), jnp.float32),
                pltpu.VMEM((2, nj, nc, vb), jnp.float32),
                pltpu.VMEM((2, va // LANES, 8, LANES), jnp.int32),
                pltpu.VMEM((turns_j, zs, 2, rows_c, m), jnp.float32),
                pltpu.VMEM((turns_j, zs, rows_c, m), jnp.float32),
                pltpu.VMEM((turns_j, zs, rows_c, m), jnp.float32),
                *bufs,
                dma((2,)),
                dma((2, nj)),
                dma((turns_j, zs)),
                dma((turns_j, zs)),
                dma((turns_j, ng, bits, zs)),
                dma((turns_j, ng, bits, zs)),
                dma((turns_j, ng, zs)),
                dma((turns_j, ng, zs)),
                dma((turns_j, ng, bits)),
                dma((turns_j, ng, bits)),
            ],
            compiler_params=pltpu.CompilerParams(
                collective_id=turn, has_side_effects=True, vmem_limit_bytes=54 * 2**20
            ),
            name="fused",
        )(occupied_irreps, slab_orbitals, amps, cycle_block, virt)
        return pl.pallas_call(
            functools.partial(unpack, cap, turn, nj),
            out_shape=jax.ShapeDtypeStruct((ni, ni, na, bw), jnp.float32),
            grid_spec=pltpu.PrefetchScalarGridSpec(
                num_scalar_prefetch=2,
                grid=(1,),
                in_specs=[
                    pl.BlockSpec((turns_j, rows_c, m), lambda k, *_: (0, 0, 0)),
                    pl.BlockSpec((va // LANES, LANES), lambda k, *_: (0, 0)),
                ],
                out_specs=pl.BlockSpec((ni, ni, na, bw), lambda k, *_: (0, 0, 0, 0)),
                scratch_shapes=[pltpu.VMEM(((-(-na // cap) + 1) * cap, bw), jnp.float32)],
            ),
            compiler_params=pltpu.CompilerParams(vmem_limit_bytes=54 * 2**20),
            name="unpack",
        )(occupied_irreps, slab_orbitals, summed, virt)

    longer = jnp.any(virtual_irreps[cap:] == virtual_irreps[:-cap])
    return lax.cond(longer, lambda x: x + part(1), lambda x: x, part(0))


def solution(mesh):
    placed = (P(None, "wide", None, "narrow"), P("wide", "narrow", None, None), P(), P(), P())
    return jax.shard_map(
        local,
        mesh=mesh,
        in_specs=placed,
        out_specs=P(None, None, "narrow", "wide"),
        check_vma=False,
    )
```

time: 211 us -> 68.9 us (0.33)
  waiting for transfers between devices: 104 us -> 0 us
  local copies, waits for them, and re-layouts: 30.2 us -> 1.07 us
  Pallas kernels: 48.6 us -> 65.1 us
  between operations: 14.1 us -> 0.73 us
  blocking collectives: 11.7 us -> 0 us
    reduce_scatter x1 -> x0, waiting for transfers between devices: 104 us -> none  [part(): lax.psum_scatter(partial_sums, ('wide', 'narrow'), scatter_dimension=0, t...]
    unnamed x5 -> x8, local copies, waits for them, and re-layouts: 20.8 us -> 1.07 us
    pallas_call x2, Pallas kernels: 48.6 us -> 65.1 us  [the longest x1 62.8 us: part(): pl.pallas_call(functools.partial(fused, cap, turn, kp, step, bits, groups...]
    all_gather x1 -> x0, blocking collectives: 11.7 us -> none  [part(): summed = lax.all_gather(mine, 'narrow', axis=0, tiled=True)]
    concatenate x2 -> x0, local copies, waits for them, and re-layouts: 3.9 us -> none  [the longest x1 1.95 us: part(): tab = jnp.concatenate([slab, occ_part, packed, c_part[:1], c_part[-1:]])]
    broadcast_in_dim x3 -> x0, local copies, waits for them, and re-layouts: 2.61 us -> none  [the longest x1 1.28 us: local(): virtual_irreps[None, :] < names[:, None]]
  transfers between devices with their start and end apart: 1 -> 0, of which waited for: 1 -> 0; matrix products, arithmetic and copies ran while one was open for 2% -> 0% of each run, Pallas kernels for 0% -> 0%
where the time goes in v3:
time: 68.9 us; the launch traced here: 68.6 us
  Pallas kernels  65.1 us (94%)
  other arithmetic  1.47 us (2%)
  local copies, waits for them, and re-layouts  1.07 us (2%)
  between operations  0.73 us (1%)
    pallas_call x1, Pallas kernels, part(): pl.pallas_call(functools.partial(fused, cap, turn, kp, step, bits, groups...  62.8 us
    pallas_call x1, Pallas kernels, part(): pl.pallas_call(functools.partial(unpack, cap, turn, nj), out_shape=jax.Sh...  2.27 us
    reduce_or x1, other arithmetic, local(): longer = jnp.any(virtual_irreps[cap:] == virtual_irreps[:-cap])  1.47 us

profile of v3, /device:TPU:0, one launch (start us, length us, event | category | flops | bytes accessed | tf_op | source)
XLA Modules:
  0.0 68.6 jit_solution(4711385160800386604)
XLA Ops:
  0.0 1.5 %fusion = pred[]{:T(512)} fusion(s32[640]{0:T(1024)} %param.10), kind=kLoop, calls=%fused_computation.1 | loop fusion | flops 1087 | bytes 4353 | tf_op jit(solution)/shard_map/reduce_or | solution.py:442
  2.1 0.0 copy-start.1
  2.1 0.0 copy-start.2
  2.1 0.0 copy-start.3
  2.2 62.8 %fused.3.g_ref = f32[2,160,384]{2,1,0:T(8,128)} custom-call(s32[64]{0:T(128)} %occ.3, s32[4]{0:T(128)} %slab.3, f32[4,8,160,640]{3,2,1,0:T(8,128)} %bitcast.2, f32[8,160,4,640]{3,2,1,0:T(4,128)} %w_ref.1, s32[5,128]{1,0:T(8,128)} %bitcast.4), custom_call_target="tpu_custom_call" | custom-call | tf_op jit(solution)/shard_map/fused/pallas_call | solution.py:385
  65.0 0.0 copy-done.1
  65.0 0.0 copy-done.2
  65.0 0.0 copy-done.3
  65.0 2.3 %unpack.3 = f32[4,4,160,80]{3,2,1,0:T(8,128)S(1)} custom-call(s32[64]{0:T(128)S(1)} %copy-done.2, s32[4]{0:T(128)S(1)} %copy-done.3, f32[2,160,384]{2,1,0:T(8,128)} %fused.3.g_ref, s32[5,128]{1,0:T(8,128)S(1)} %bitcast.5), custom_call_target="tpu_custom_call" | custom-call | tf_op jit(solution)/shard_map/unpack/pallas_call | solution.py:425
  67.3 0.2 conditional.1
  67.5 0.0 copy-start
  67.5 1.0 %copy-done = f32[4,4,160,80]{3,2,1,0:T(8,128)} copy-done((f32[4,4,160,80]{3,2,1,0:T(8,128)}, f32[4,4,160,80]{3,2,1,0:T(8,128)S(1)}, u32[]{:S(2)}) %copy-start) | copy-done | bytes 819224
Async XLA Ops:
  2.1 62.9 %copy-start.1 = (s32[640]{0:T(1024)S(1)}, s32[640]{0:T(1024)}, u32[]{:S(2)}) copy-start(s32[640]{0:T(1024)} %param.10) | copy-start | bytes 7684
  2.1 62.9 %copy-start.2 = (s32[64]{0:T(128)S(1)}, s32[64]{0:T(128)}, u32[]{:S(2)}) copy-start(s32[64]{0:T(128)} %occ.3) | copy-start | bytes 772
  2.1 62.9 %copy-start.3 = (s32[4]{0:T(128)S(1)}, s32[4]{0:T(128)}, u32[]{:S(2)}) copy-start(s32[4]{0:T(128)} %slab.3) | copy-start | bytes 52
  67.5 1.1 %copy-start = (f32[4,4,160,80]{3,2,1,0:T(8,128)}, f32[4,4,160,80]{3,2,1,0:T(8,128)S(1)}, u32[]{:S(2)}) copy-start(f32[4,4,160,80]{3,2,1,0:T(8,128)S(1)} %get-tuple-element.30) | copy-start | bytes 2457604

commit v4 on v3

--- a/solution.py
+++ b/solution.py
@@ -41,6 +41,41 @@
         first = jnp.where(index >= start, start, first)
     place = index - first
     return jnp.where((place >= turn * cap) & (place < (turn + 1) * cap), label, 8 * IRREPS)
+
+
+def folded(tiles, turns, first, last, lane):
+    n_t, made = len(tiles), {}
+
+    def turned(level, t):
+        if level == 0:
+            return tiles[t % n_t]
+        if (level, t % n_t) not in made:
+            made[level, t % n_t] = whole(level, t % n_t, 0, LANES)
+        return made[level, t % n_t]
+
+    def rolled(level, t, by):
+        key = (level, t % n_t, by, "rolled")
+        if key not in made:
+            x = turned(level, t)
+            made[key] = pltpu.roll(x, by, axis=1) if by else x
+        return made[key]
+
+    def whole(level, t, low, high):
+        tiles_back, by = divmod(turns[level - 1], LANES)
+        if low >= by:
+            moved = rolled(level - 1, t - tiles_back, by)
+        elif high <= by:
+            moved = rolled(level - 1, t - tiles_back - 1, by)
+        else:
+            near, far = rolled(level - 1, t - tiles_back, by), rolled(level - 1, t - tiles_back - 1, by)
+            moved = jnp.where(lane < by, far, near)
+        return turned(level - 1, t) + moved
+
+    out = []
+    for t in range(n_t):
+        low, high = max(first - t * LANES, 0), min(last - t * LANES, LANES)
+        out.append(whole(len(turns), t, low, high) if low < high else None)
+    return out
 
 
 def fused(cap, turn, kp, step, bits, groups, segments, occ, slab, a_ref, w_ref, v_ref, out_ref, *rest):
@@ -96,27 +131,27 @@
     slab_labels = [occ[slab[i]] for i in range(ni)]
 
     def build_a(own, slot, r):
-        lane = lax.broadcasted_iota(jnp.int32, (step, m), 1)
+        lane = lax.broadcasted_iota(jnp.int32, (step, LANES), 1)
         at = pl.multiple_of(r * step, step)
         rows = pl.ds(at, step)
         hcr = hc[rows, :].reshape(step // 8, 8, LANES)
-        kept = None
+        n_t = m // LANES
+        kept = [None] * n_t
         for i in range(ni):
             g = hcr ^ own[i]
-            tiles = []
-            for t in range(m // LANES):
+            x = []
+            for t in range(n_t):
                 tile = jnp.zeros((step, LANES), jnp.float32)
-                for s in range(t, va // LANES, m // LANES):
+                for s in range(t, va // LANES, n_t):
                     mask = (g == labs[0, s][None]).reshape(step, LANES)
                     tile = jnp.where(mask, tbuf[slot, i, rows, s * LANES : (s + 1) * LANES], tile)
-                tiles.append(tile)
-            x = jnp.concatenate(tiles, axis=1)
-            turns = ni // 2
-            while turns:
-                x = x + pltpu.roll(x, turns * cap, axis=1)
-                turns //= 2
-            kept = x if kept is None else jnp.where(lane >= i * cap, x, kept)
-        hi, lo = split(kept)
+                x.append(tile)
+            turns = [(ni >> n) * cap for n in range(1, ni.bit_length())]
+            x = folded(x, turns, i * cap, (i + 1) * cap, lane)
+            for t in range(n_t):
+                if x[t] is not None:
+                    kept[t] = x[t] if kept[t] is None else jnp.where(lane >= i * cap - t * LANES, x[t], kept[t])
+        hi, lo = split(jnp.concatenate(kept, axis=1))
         for p, part in enumerate((hi, hi, lo)):
             lcat[pl.ds(p * kp + at, step), :] = part
 
@@ -167,8 +202,8 @@
         lax.fori_loop(0, nc // step, rows_of, 0)
         if turn_j == 0:
             lt[k] = lcat[...].T
-        for c in range(0, nj * vb, 2 * LANES):
-            cols = slice(c, c + 2 * LANES)
+        for c in range(0, nj * vb, 4 * LANES):
+            cols = slice(c, min(c + 4 * LANES, nj * vb))
             acc[:, cols] += jnp.dot(lt[k], wcat[:, cols], preferred_element_type=jnp.float32)
 
     def some_k(first, last, turn_j):

time: 68.9 us -> 68.1 us (0.988)
  Pallas kernels: 65.1 us -> 64.3 us
    pallas_call x1, Pallas kernels: 62.8 us -> 62 us  [part(): pl.pallas_call(functools.partial(fused, cap, turn, kp, step, bits, groups...]
where the time goes in v4:
time: 68.1 us; the launch traced here: 67.8 us
  Pallas kernels  64.3 us (94%)
  other arithmetic  1.47 us (2%)
  local copies, waits for them, and re-layouts  1.07 us (2%)
  between operations  0.73 us (1%)
    pallas_call x1, Pallas kernels, part(): pl.pallas_call(functools.partial(fused, cap, turn, kp, step, bits, groups...  62 us
    pallas_call x1, Pallas kernels, part(): pl.pallas_call(functools.partial(unpack, cap, turn, nj), out_shape=jax.Sh...  2.27 us
    reduce_or x1, other arithmetic, local(): longer = jnp.any(virtual_irreps[cap:] == virtual_irreps[:-cap])  1.47 us

profile of v4, /device:TPU:0, one launch (start us, length us, event | category | flops | bytes accessed | tf_op | source)
XLA Modules:
  0.0 67.8 jit_solution(11836097134437886258)
XLA Ops:
  0.0 1.5 %fusion = pred[]{:T(512)} fusion(s32[640]{0:T(1024)} %param.10), kind=kLoop, calls=%fused_computation.1 | loop fusion | flops 1087 | bytes 4353 | tf_op jit(solution)/shard_map/reduce_or | solution.py:477
  2.1 0.0 copy-start.1
  2.1 0.0 copy-start.2
  2.1 0.0 copy-start.3
  2.2 62.0 %fused.3.g_ref = f32[2,160,384]{2,1,0:T(8,128)} custom-call(s32[64]{0:T(128)} %occ.3, s32[4]{0:T(128)} %slab.3, f32[4,8,160,640]{3,2,1,0:T(8,128)} %bitcast.2, f32[8,160,4,640]{3,2,1,0:T(4,128)} %w_ref.1, s32[5,128]{1,0:T(8,128)} %bitcast.4), custom_call_target="tpu_custom_call" | custom-call | tf_op jit(solution)/shard_map/fused/pallas_call | solution.py:420
  64.2 0.0 copy-done.1
  64.2 0.0 copy-done.2
  64.2 0.0 copy-done.3
  64.2 2.3 %unpack.3 = f32[4,4,160,80]{3,2,1,0:T(8,128)S(1)} custom-call(s32[64]{0:T(128)S(1)} %copy-done.2, s32[4]{0:T(128)S(1)} %copy-done.3, f32[2,160,384]{2,1,0:T(8,128)} %fused.3.g_ref, s32[5,128]{1,0:T(8,128)S(1)} %bitcast.5), custom_call_target="tpu_custom_call" | custom-call | tf_op jit(solution)/shard_map/unpack/pallas_call | solution.py:460
  66.5 0.2 conditional.1
  66.7 0.0 copy-start
  66.7 1.0 %copy-done = f32[4,4,160,80]{3,2,1,0:T(8,128)} copy-done((f32[4,4,160,80]{3,2,1,0:T(8,128)}, f32[4,4,160,80]{3,2,1,0:T(8,128)S(1)}, u32[]{:S(2)}) %copy-start) | copy-done | bytes 819224
Async XLA Ops:
  2.1 62.1 %copy-start.1 = (s32[640]{0:T(1024)S(1)}, s32[640]{0:T(1024)}, u32[]{:S(2)}) copy-start(s32[640]{0:T(1024)} %param.10) | copy-start | bytes 7684
  2.1 62.1 %copy-start.2 = (s32[64]{0:T(128)S(1)}, s32[64]{0:T(128)}, u32[]{:S(2)}) copy-start(s32[64]{0:T(128)} %occ.3) | copy-start | bytes 772
  2.1 62.1 %copy-start.3 = (s32[4]{0:T(128)S(1)}, s32[4]{0:T(128)}, u32[]{:S(2)}) copy-start(s32[4]{0:T(128)} %slab.3) | copy-start | bytes 52
  66.7 1.1 %copy-start = (f32[4,4,160,80]{3,2,1,0:T(8,128)}, f32[4,4,160,80]{3,2,1,0:T(8,128)S(1)}, u32[]{:S(2)}) copy-start(f32[4,4,160,80]{3,2,1,0:T(8,128)S(1)} %get-tuple-element.30) | copy-start | bytes 2457604

commit v5 on v4

--- a/solution.py
+++ b/solution.py
@@ -347,10 +347,11 @@
     next(trips[0])
     for q in range(1, turns_j):
         acc[...] = jnp.zeros_like(acc)
-        for at in range(segments):
-            some_k(at * n_k // segments, (at + 1) * n_k // segments, q)
-            if at + 1 < segments:
+        cuts = [0, *(n_k * part // 8 for part in segments), n_k]
+        for first, last in zip(cuts, cuts[1:]):
+            if first:
                 next(trips[0], None)
+            some_k(first, last, q)
         hand_over(q)
         trips.append(travel(q))
         next(trips[q])
@@ -418,7 +419,7 @@
 
     def part(turn):
         summed = pl.pallas_call(
-            functools.partial(fused, cap, turn, kp, step, bits, groups, 4),
+            functools.partial(fused, cap, turn, kp, step, bits, groups, (3,)),
             out_shape=jax.ShapeDtypeStruct((turns_j, rows_c, m), jnp.float32),
             in_specs=[
                 pl.BlockSpec(memory_space=pltpu.SMEM),

time: 68.1 us -> 64.5 us (0.947)
  Pallas kernels: 64.3 us -> 60.8 us
    pallas_call x1, Pallas kernels: 62 us -> 58.6 us  [part(): pl.pallas_call(functools.partial(fused, cap, turn, kp, step, bits, groups...]
where the time goes in v5:
time: 64.5 us; the launch traced here: 64.1 us
  Pallas kernels  60.8 us (94%)
  other arithmetic  1.47 us (2%)
  local copies, waits for them, and re-layouts  1.07 us (2%)
  between operations  0.73 us (1%)
    pallas_call x1, Pallas kernels, part(): pl.pallas_call(functools.partial(fused, cap, turn, kp, step, bits, groups...  58.6 us
    pallas_call x1, Pallas kernels, part(): pl.pallas_call(functools.partial(unpack, cap, turn, nj), out_shape=jax.Sh...  2.27 us
    reduce_or x1, other arithmetic, local(): longer = jnp.any(virtual_irreps[cap:] == virtual_irreps[:-cap])  1.47 us

profile of v5, /device:TPU:0, one launch (start us, length us, event | category | flops | bytes accessed | tf_op | source)
XLA Modules:
  0.0 64.1 jit_solution(7585837079605987597)
XLA Ops:
  0.0 1.5 %fusion = pred[]{:T(512)} fusion(s32[640]{0:T(1024)} %param.10), kind=kLoop, calls=%fused_computation.1 | loop fusion | flops 1087 | bytes 4353 | tf_op jit(solution)/shard_map/reduce_or | solution.py:478
  2.1 0.0 copy-start.1
  2.1 0.0 copy-start.2
  2.1 0.0 copy-start.3
  2.2 58.6 %fused.3.g_ref = f32[2,160,384]{2,1,0:T(8,128)} custom-call(s32[64]{0:T(128)} %occ.3, s32[4]{0:T(128)} %slab.3, f32[4,8,160,640]{3,2,1,0:T(8,128)} %bitcast.2, f32[8,160,4,640]{3,2,1,0:T(4,128)} %w_ref.1, s32[5,128]{1,0:T(8,128)} %bitcast.4), custom_call_target="tpu_custom_call" | custom-call | tf_op jit(solution)/shard_map/fused/pallas_call | solution.py:421
  60.7 0.0 copy-done.1
  60.7 0.0 copy-done.2
  60.7 0.0 copy-done.3
  60.8 2.3 %unpack.3 = f32[4,4,160,80]{3,2,1,0:T(8,128)S(1)} custom-call(s32[64]{0:T(128)S(1)} %copy-done.2, s32[4]{0:T(128)S(1)} %copy-done.3, f32[2,160,384]{2,1,0:T(8,128)} %fused.3.g_ref, s32[5,128]{1,0:T(8,128)S(1)} %bitcast.5), custom_call_target="tpu_custom_call" | custom-call | tf_op jit(solution)/shard_map/unpack/pallas_call | solution.py:461
  63.0 0.0 copy-start
  63.1 1.0 %copy-done = f32[4,4,160,80]{3,2,1,0:T(8,128)} copy-done((f32[4,4,160,80]{3,2,1,0:T(8,128)}, f32[4,4,160,80]{3,2,1,0:T(8,128)S(1)}, u32[]{:S(2)}) %copy-start) | copy-done | bytes 819224
  (1 shorter events, 0.0 us)
Async XLA Ops:
  2.1 58.6 %copy-start.1 = (s32[640]{0:T(1024)S(1)}, s32[640]{0:T(1024)}, u32[]{:S(2)}) copy-start(s32[640]{0:T(1024)} %param.10) | copy-start | bytes 7684
  2.1 58.6 %copy-start.2 = (s32[64]{0:T(128)S(1)}, s32[64]{0:T(128)}, u32[]{:S(2)}) copy-start(s32[64]{0:T(128)} %occ.3) | copy-start | bytes 772
  2.1 58.6 %copy-start.3 = (s32[4]{0:T(128)S(1)}, s32[4]{0:T(128)}, u32[]{:S(2)}) copy-start(s32[4]{0:T(128)} %slab.3) | copy-start | bytes 52
  63.0 1.1 %copy-start = (f32[4,4,160,80]{3,2,1,0:T(8,128)}, f32[4,4,160,80]{3,2,1,0:T(8,128)S(1)}, u32[]{:S(2)}) copy-start(f32[4,4,160,80]{3,2,1,0:T(8,128)S(1)} %get-tuple-element.30) | copy-start | bytes 2457604

commit v6 on v5

--- a/solution.py
+++ b/solution.py
@@ -352,6 +352,7 @@
             if first:
                 next(trips[0], None)
             some_k(first, last, q)
+        next(trips[0], None)
         hand_over(q)
         trips.append(travel(q))
         next(trips[q])

time: 64.5 us -> 66.2 us (1.026)
  Pallas kernels: 60.8 us -> 62.5 us
    pallas_call x1, Pallas kernels: 58.6 us -> 60.3 us  [part(): pl.pallas_call(functools.partial(fused, cap, turn, kp, step, bits, groups...]
where the time goes in v6:
time: 66.2 us; the launch traced here: 65.8 us
  Pallas kernels  62.5 us (94%)
  other arithmetic  1.47 us (2%)
  local copies, waits for them, and re-layouts  1.07 us (2%)
  between operations  0.73 us (1%)
    pallas_call x1, Pallas kernels, part(): pl.pallas_call(functools.partial(fused, cap, turn, kp, step, bits, groups...  60.3 us
    pallas_call x1, Pallas kernels, part(): pl.pallas_call(functools.partial(unpack, cap, turn, nj), out_shape=jax.Sh...  2.27 us
    reduce_or x1, other arithmetic, local(): longer = jnp.any(virtual_irreps[cap:] == virtual_irreps[:-cap])  1.47 us

profile of v6, /device:TPU:0, one launch (start us, length us, event | category | flops | bytes accessed | tf_op | source)
XLA Modules:
  0.0 65.8 jit_solution(7244399588531681098)
XLA Ops:
  0.0 1.5 %fusion = pred[]{:T(512)} fusion(s32[640]{0:T(1024)} %param.10), kind=kLoop, calls=%fused_computation.1 | loop fusion | flops 1087 | bytes 4353 | tf_op jit(solution)/shard_map/reduce_or | solution.py:479
  2.1 0.0 copy-start.1
  2.1 0.0 copy-start.2
  2.1 0.0 copy-start.3
  2.2 60.3 %fused.3.g_ref = f32[2,160,384]{2,1,0:T(8,128)} custom-call(s32[64]{0:T(128)} %occ.3, s32[4]{0:T(128)} %slab.3, f32[4,8,160,640]{3,2,1,0:T(8,128)} %bitcast.2, f32[8,160,4,640]{3,2,1,0:T(4,128)} %w_ref.1, s32[5,128]{1,0:T(8,128)} %bitcast.4), custom_call_target="tpu_custom_call" | custom-call | tf_op jit(solution)/shard_map/fused/pallas_call | solution.py:422
  62.4 0.0 copy-done.1
  62.4 0.0 copy-done.2
  62.5 0.0 copy-done.3
  62.5 2.3 %unpack.3 = f32[4,4,160,80]{3,2,1,0:T(8,128)S(1)} custom-call(s32[64]{0:T(128)S(1)} %copy-done.2, s32[4]{0:T(128)S(1)} %copy-done.3, f32[2,160,384]{2,1,0:T(8,128)} %fused.3.g_ref, s32[5,128]{1,0:T(8,128)S(1)} %bitcast.5), custom_call_target="tpu_custom_call" | custom-call | tf_op jit(solution)/shard_map/unpack/pallas_call | solution.py:462
  64.8 0.0 copy-start
  64.8 1.0 %copy-done = f32[4,4,160,80]{3,2,1,0:T(8,128)} copy-done((f32[4,4,160,80]{3,2,1,0:T(8,128)}, f32[4,4,160,80]{3,2,1,0:T(8,128)S(1)}, u32[]{:S(2)}) %copy-start) | copy-done | bytes 819224
  (1 shorter events, 0.0 us)
Async XLA Ops:
  2.1 60.3 %copy-start.1 = (s32[640]{0:T(1024)S(1)}, s32[640]{0:T(1024)}, u32[]{:S(2)}) copy-start(s32[640]{0:T(1024)} %param.10) | copy-start | bytes 7684
  2.1 60.3 %copy-start.2 = (s32[64]{0:T(128)S(1)}, s32[64]{0:T(128)}, u32[]{:S(2)}) copy-start(s32[64]{0:T(128)} %occ.3) | copy-start | bytes 772
  2.1 60.3 %copy-start.3 = (s32[4]{0:T(128)S(1)}, s32[4]{0:T(128)}, u32[]{:S(2)}) copy-start(s32[4]{0:T(128)} %slab.3) | copy-start | bytes 52
  64.8 1.1 %copy-start = (f32[4,4,160,80]{3,2,1,0:T(8,128)}, f32[4,4,160,80]{3,2,1,0:T(8,128)S(1)}, u32[]{:S(2)}) copy-start(f32[4,4,160,80]{3,2,1,0:T(8,128)S(1)} %get-tuple-element.30) | copy-start | bytes 2457604
